TPU v7x, 32 devices: a whole 2x2x4 slice. The times are simulated.
32 devices in a mesh: replica: 2 (over y), fsdp: 8 (over z, core), seq: 2 (over x).
Axes of the slice: x: 2, y: 2, z: 4, core: 2. Of those that a mesh axis runs over, the one named last changes fastest.
Arguments:
- series_in: bfloat16 [16, 512, 1280], P(('replica', 'fsdp'), 'seq'), may hold values from -6 to 6
- cotangent: bfloat16 [16, 512, 1280], P(('replica', 'fsdp'), 'seq'), may hold values from -6 to 6
- qkv_weight: bfloat16 [2, 1280, 3840], P(None, 'fsdp'), may hold values from -0.15625 to 0.15625
- out_weight: bfloat16 [2, 1280, 1280], P(None, 'fsdp'), may hold values from -0.625 to 0.625
- up_weight: bfloat16 [2, 1280, 1280], P(None, 'fsdp'), may hold values from -0.15625 to 0.15625
- down_weight: bfloat16 [2, 1280, 1280], P(None, 'fsdp'), may hold values from -0.15625 to 0.15625
- norm_gains: bfloat16 [2, 2, 1280], P(None, None, 'fsdp'), may hold values from 0.25 to 1.75
- up_bias: bfloat16 [2, 1280], P(None, 'fsdp'), may hold values from -3 to 3
- down_bias: bfloat16 [2, 1280], P(None, 'fsdp'), may hold values from -2 to 2
- query_scale: bfloat16 [2, 80], P(None, 'fsdp'), may hold values from -1 to 1
- pad_length: int32 [16], P(('replica', 'fsdp')), may hold values from 0 to 128, as said below
- span_starts: int32 [16, 4], P(('replica', 'fsdp')), may hold values from 0 to 480, as said below
- span_count: int32 [16], P(('replica', 'fsdp')), may hold values from 1 to 4, as said below
Outputs:
- series_out: bfloat16 [16, 512, 1280], P(('replica', 'fsdp'), 'seq')
- input_grad: bfloat16 [16, 512, 1280], P(('replica', 'fsdp'), 'seq')
- grad_qkv: float32 [2, 1280, 3840], P(None, 'fsdp')
- grad_out: float32 [2, 1280, 1280], P(None, 'fsdp')
- grad_up: float32 [2, 1280, 1280], P(None, 'fsdp')
- grad_down: float32 [2, 1280, 1280], P(None, 'fsdp')
- grad_gains: float32 [2, 2, 1280], P(None, None, 'fsdp')
- grad_up_bias: float32 [2, 1280], P(None, 'fsdp')
- grad_down_bias: float32 [2, 1280], P(None, 'fsdp')
- grad_query_scale: float32 [2, 80], P(None, 'fsdp')
Inputs may be any that keep to these rules, and one draw needn't show every extreme that they name: `pad_length`: one series in every draw has exactly 128 padded positions. `span_starts`: slot 0 of every series starts within 31 positions before 256, so it holds positions 255 and 256; spans may intersect. Slot k of series b is used when k < span_count[b].
All inputs are finite; a program needn't handle non-finite values.
Results may differ from a plain program's by a relative error of at most 0.025.
Values may be sent and summed in bfloat16 or wider, within the bound.
A program may use at most 256 MiB of HBM per device.

v0:
```python
import math
import jax
import jax.numpy as jnp
from jax import lax
from jax.sharding import PartitionSpec as P

HEADS = 16
HEAD = 80
SPAN = 32
EPSILON = 1e-06
SOFT_ONE = 1.442695041
NEG_FILL = -1e30


def visible(pad_length, span_starts, span_count, offset, local_length, total_length):
    query_pos = offset + jnp.arange(local_length, dtype=jnp.int32)
    key_pos = jnp.arange(total_length, dtype=jnp.int32)
    shared = jnp.zeros((span_starts.shape[0], local_length, total_length), dtype=bool)
    for slot_index in range(span_starts.shape[1]):
        slot_start = span_starts[:, slot_index]
        slot_used = slot_index < span_count
        query_in = (
            slot_used[:, None]
            & (query_pos[None, :] >= slot_start[:, None])
            & (query_pos[None, :] < slot_start[:, None] + SPAN)
        )
        key_in = (key_pos[None, :] >= slot_start[:, None]) & (
            key_pos[None, :] < slot_start[:, None] + SPAN
        )
        shared = shared | query_in[:, :, None] & key_in[:, None, :]
    causal = key_pos[None, :] <= query_pos[:, None]
    allowed = (key_pos[None, None, :] >= pad_length[:, None, None]) & (causal[None] | shared)
    return allowed | (key_pos[None, None, :] == query_pos[None, :, None])


def norm_rows(values, scale_gain):
    inverse = lax.rsqrt(jnp.mean(values * values, axis=-1, keepdims=True) + EPSILON)
    return (values * inverse * scale_gain, inverse)


def norm_back(values, inverse, scale_gain, upstream):
    scaled = upstream * scale_gain
    inner_term = jnp.mean(values * scaled, axis=-1, keepdims=True)
    result = inverse * scaled - values * (inverse * inverse * inverse) * inner_term
    return (result, jnp.sum(upstream * values * inverse, axis=0))


def query_factor(query_scale):
    return jax.nn.softplus(query_scale.astype(jnp.float32)) * (SOFT_ONE / math.sqrt(HEAD))


def forward_layer(current, weights, allowed, series_count, local_length, total_length):
    qkv_weight, out_weight, up_weight, down_weight, norm_gains, up_bias, down_bias, query_scale = (
        weights
    )
    token_count, model_width = current.shape
    normed, inverse_one = norm_rows(current, norm_gains[0].astype(jnp.float32))
    normed_low = normed.astype(jnp.bfloat16).reshape(series_count, local_length, model_width)
    projected = jnp.einsum(
        "bld,dc->bcl", normed_low, qkv_weight, preferred_element_type=jnp.float32
    )
    query_raw = projected[:, :model_width]
    factor = query_factor(query_scale)
    query_low = (
        query_raw.reshape(series_count, HEADS, HEAD, local_length) * factor[None, None, :, None]
    ).astype(jnp.bfloat16)
    pair_low = projected[:, model_width:].astype(jnp.bfloat16)
    pair_all = lax.all_gather(pair_low, "seq", axis=2, tiled=True)
    key_all = pair_all[:, :model_width].reshape(series_count, HEADS, HEAD, total_length)
    value_all = pair_all[:, model_width:].reshape(series_count, HEADS, HEAD, total_length)
    scores = jnp.einsum("bheq,bhek->bhqk", query_low, key_all, preferred_element_type=jnp.float32)
    scores = jnp.where(allowed[:, None], scores, NEG_FILL)
    top_score = jnp.max(scores, axis=-1, keepdims=True)
    exp_scores = jnp.exp(scores - top_score)
    exp_total = jnp.sum(exp_scores, axis=-1, keepdims=True)
    probs_low = (exp_scores / exp_total).astype(jnp.bfloat16)
    log_total = top_score + jnp.log(exp_total)
    attended = jnp.einsum(
        "bhqk,bhek->bheq", probs_low, value_all, preferred_element_type=jnp.float32
    )
    attended_low = attended.astype(jnp.bfloat16).reshape(series_count, model_width, local_length)
    attn_out = jnp.einsum(
        "bdl,de->ble", attended_low, out_weight, preferred_element_type=jnp.float32
    )
    after_attn = current + attn_out.reshape(token_count, model_width)
    normed_two, inverse_two = norm_rows(after_attn, norm_gains[1].astype(jnp.float32))
    mixed_low = normed_two.astype(jnp.bfloat16)
    hidden_pre = jnp.dot(mixed_low, up_weight, preferred_element_type=jnp.float32) + up_bias.astype(
        jnp.float32
    )
    hidden_low = jax.nn.silu(hidden_pre).astype(jnp.bfloat16)
    result = after_attn + (
        jnp.dot(hidden_low, down_weight, preferred_element_type=jnp.float32)
        + down_bias.astype(jnp.float32)
    )
    stored = (
        current,
        inverse_one,
        normed_low,
        query_raw,
        query_low,
        key_all,
        value_all,
        log_total,
        attended_low,
        after_attn,
        inverse_two,
        mixed_low,
        hidden_pre,
        hidden_low,
    )
    return (result, stored)


def backward_layer(upstream, weights, stored, allowed, series_count, local_length, total_length):
    qkv_weight, out_weight, up_weight, down_weight, norm_gains, up_bias, down_bias, query_scale = (
        weights
    )
    (
        current,
        inverse_one,
        normed_low,
        query_raw,
        query_low,
        key_all,
        value_all,
        log_total,
        attended_low,
        after_attn,
        inverse_two,
        mixed_low,
        hidden_pre,
        hidden_low,
    ) = stored
    token_count, model_width = current.shape
    down_low = upstream.astype(jnp.bfloat16)
    grad_down_bias = jnp.sum(down_low, axis=0, dtype=jnp.float32)
    grad_down = jnp.einsum("tf,td->fd", hidden_low, down_low, preferred_element_type=jnp.float32)
    hidden_grad = jnp.einsum("td,fd->tf", down_low, down_weight, preferred_element_type=jnp.float32)
    sigmoid_pre = jax.nn.sigmoid(hidden_pre)
    pre_low = (hidden_grad * sigmoid_pre * (1.0 + hidden_pre * (1.0 - sigmoid_pre))).astype(
        jnp.bfloat16
    )
    grad_up_bias = jnp.sum(pre_low, axis=0, dtype=jnp.float32)
    grad_up = jnp.einsum("td,tf->df", mixed_low, pre_low, preferred_element_type=jnp.float32)
    mixed_grad = jnp.einsum("tf,df->td", pre_low, up_weight, preferred_element_type=jnp.float32)
    norm_grad_two, gain_grad_two = norm_back(
        after_attn, inverse_two, norm_gains[1].astype(jnp.float32), mixed_grad
    )
    attn_grad = upstream + norm_grad_two
    branch_low = attn_grad.astype(jnp.bfloat16).reshape(series_count, local_length, model_width)
    grad_out = jnp.einsum(
        "bdl,ble->de", attended_low, branch_low, preferred_element_type=jnp.float32
    )
    output_low = (
        jnp.einsum("ble,de->bdl", branch_low, out_weight, preferred_element_type=jnp.float32)
        .astype(jnp.bfloat16)
        .reshape(series_count, HEADS, HEAD, local_length)
    )
    scores = jnp.einsum("bheq,bhek->bhqk", query_low, key_all, preferred_element_type=jnp.float32)
    scores = jnp.where(allowed[:, None], scores, NEG_FILL)
    attn_probs = jnp.exp(scores - log_total)
    prob_grad = jnp.einsum(
        "bheq,bhek->bhqk", output_low, value_all, preferred_element_type=jnp.float32
    )
    row_inner = jnp.sum(attn_probs * prob_grad, axis=-1, keepdims=True)
    score_low = (attn_probs * (prob_grad - row_inner)).astype(jnp.bfloat16)
    value_grad = jnp.einsum(
        "bhqk,bheq->bhek",
        attn_probs.astype(jnp.bfloat16),
        output_low,
        preferred_element_type=jnp.float32,
    )
    key_grad = jnp.einsum(
        "bhqk,bheq->bhek", score_low, query_low, preferred_element_type=jnp.float32
    )
    query_grad = jnp.einsum(
        "bhqk,bhek->bheq", score_low, key_all, preferred_element_type=jnp.float32
    )
    key_local, value_local = (
        lax.psum_scatter(
            key_grad.reshape(series_count, model_width, total_length),
            "seq",
            scatter_dimension=2,
            tiled=True,
        ),
        lax.psum_scatter(
            value_grad.reshape(series_count, model_width, total_length),
            "seq",
            scatter_dimension=2,
            tiled=True,
        ),
    )
    factor = query_factor(query_scale)
    factor_grad = jnp.sum(
        query_grad * query_raw.reshape(series_count, HEADS, HEAD, local_length), axis=(0, 1, 3)
    )
    grad_scale = (
        factor_grad * jax.nn.sigmoid(query_scale.astype(jnp.float32)) * (SOFT_ONE / math.sqrt(HEAD))
    )
    raw_low = (
        (query_grad * factor[None, None, :, None])
        .astype(jnp.bfloat16)
        .reshape(series_count, model_width, local_length)
    )
    projected_grad = jnp.concatenate(
        [raw_low, key_local.astype(jnp.bfloat16), value_local.astype(jnp.bfloat16)], axis=1
    )
    grad_qkv = jnp.einsum(
        "bld,bcl->dc", normed_low, projected_grad, preferred_element_type=jnp.float32
    )
    normed_grad = jnp.einsum(
        "bcl,dc->bld", projected_grad, qkv_weight, preferred_element_type=jnp.float32
    ).reshape(token_count, model_width)
    norm_grad_one, gain_grad_one = norm_back(
        current, inverse_one, norm_gains[0].astype(jnp.float32), normed_grad
    )
    result = attn_grad + norm_grad_one
    layer_grads = (
        grad_qkv,
        grad_out,
        grad_up,
        grad_down,
        jnp.stack([gain_grad_one, gain_grad_two]),
        grad_up_bias,
        grad_down_bias,
        grad_scale,
    )
    return (result, layer_grads)


def shards(
    series_in,
    cotangent,
    qkv_weight,
    out_weight,
    up_weight,
    down_weight,
    norm_gains,
    up_bias,
    down_bias,
    query_scale,
    pad_length,
    span_starts,
    span_count,
):
    series_count, local_length, model_width = series_in.shape
    seq_count = lax.axis_size("seq")
    total_length = local_length * seq_count
    offset = lax.axis_index("seq") * local_length
    allowed = visible(pad_length, span_starts, span_count, offset, local_length, total_length)
    layer_count = qkv_weight.shape[0]
    current = series_in.reshape(series_count * local_length, model_width).astype(jnp.float32)
    gathered_list = []
    stored_list = []
    for layer_index in range(layer_count):
        gathered = (
            lax.all_gather(qkv_weight[layer_index], "fsdp", axis=0, tiled=True),
            lax.all_gather(out_weight[layer_index], "fsdp", axis=0, tiled=True),
            lax.all_gather(up_weight[layer_index], "fsdp", axis=0, tiled=True),
            lax.all_gather(down_weight[layer_index], "fsdp", axis=0, tiled=True),
            lax.all_gather(norm_gains[layer_index], "fsdp", axis=1, tiled=True),
            lax.all_gather(up_bias[layer_index], "fsdp", axis=0, tiled=True),
            lax.all_gather(down_bias[layer_index], "fsdp", axis=0, tiled=True),
            lax.all_gather(query_scale[layer_index], "fsdp", axis=0, tiled=True),
        )
        current, stored = forward_layer(
            current, gathered, allowed, series_count, local_length, total_length
        )
        gathered_list.append(gathered)
        stored_list.append(stored)
    series_out = current.reshape(series_count, local_length, model_width).astype(jnp.bfloat16)
    upstream = cotangent.reshape(series_count * local_length, model_width).astype(jnp.float32)
    owned_list = [None] * layer_count
    for layer_index in reversed(range(layer_count)):
        gathered = (
            lax.all_gather(qkv_weight[layer_index], "fsdp", axis=0, tiled=True),
            lax.all_gather(out_weight[layer_index], "fsdp", axis=0, tiled=True),
            lax.all_gather(up_weight[layer_index], "fsdp", axis=0, tiled=True),
            lax.all_gather(down_weight[layer_index], "fsdp", axis=0, tiled=True),
            lax.all_gather(norm_gains[layer_index], "fsdp", axis=1, tiled=True),
            lax.all_gather(up_bias[layer_index], "fsdp", axis=0, tiled=True),
            lax.all_gather(down_bias[layer_index], "fsdp", axis=0, tiled=True),
            lax.all_gather(query_scale[layer_index], "fsdp", axis=0, tiled=True),
        )
        upstream, layer_grads = backward_layer(
            upstream,
            gathered,
            stored_list[layer_index],
            allowed,
            series_count,
            local_length,
            total_length,
        )
        shares = (
            lax.psum_scatter(
                layer_grads[0].astype(jnp.bfloat16), "fsdp", scatter_dimension=0, tiled=True
            ).astype(jnp.float32),
            lax.psum_scatter(
                layer_grads[1].astype(jnp.bfloat16), "fsdp", scatter_dimension=0, tiled=True
            ).astype(jnp.float32),
            lax.psum_scatter(
                layer_grads[2].astype(jnp.bfloat16), "fsdp", scatter_dimension=0, tiled=True
            ).astype(jnp.float32),
            lax.psum_scatter(
                layer_grads[3].astype(jnp.bfloat16), "fsdp", scatter_dimension=0, tiled=True
            ).astype(jnp.float32),
            lax.psum_scatter(
                layer_grads[4].astype(jnp.bfloat16), "fsdp", scatter_dimension=1, tiled=True
            ).astype(jnp.float32),
            lax.psum_scatter(
                layer_grads[5].astype(jnp.bfloat16), "fsdp", scatter_dimension=0, tiled=True
            ).astype(jnp.float32),
            lax.psum_scatter(
                layer_grads[6].astype(jnp.bfloat16), "fsdp", scatter_dimension=0, tiled=True
            ).astype(jnp.float32),
            lax.psum_scatter(
                layer_grads[7].astype(jnp.bfloat16), "fsdp", scatter_dimension=0, tiled=True
            ).astype(jnp.float32),
        )
        shares = (
            lax.psum(shares[0].astype(jnp.bfloat16), ("replica", "seq")).astype(jnp.float32),
            lax.psum(shares[1].astype(jnp.bfloat16), ("replica", "seq")).astype(jnp.float32),
            lax.psum(shares[2].astype(jnp.bfloat16), ("replica", "seq")).astype(jnp.float32),
            lax.psum(shares[3].astype(jnp.bfloat16), ("replica", "seq")).astype(jnp.float32),
            lax.psum(shares[4].astype(jnp.bfloat16), ("replica", "seq")).astype(jnp.float32),
            lax.psum(shares[5].astype(jnp.bfloat16), ("replica", "seq")).astype(jnp.float32),
            lax.psum(shares[6].astype(jnp.bfloat16), ("replica", "seq")).astype(jnp.float32),
            lax.psum(shares[7].astype(jnp.bfloat16), ("replica", "seq")).astype(jnp.float32),
        )
        owned_list[layer_index] = shares
    stacked = [
        jnp.stack([owned_list[layer_index][member_index] for layer_index in range(layer_count)])
        for member_index in range(8)
    ]
    input_grad = upstream.reshape(series_count, local_length, model_width).astype(jnp.bfloat16)
    return (
        series_out,
        input_grad,
        stacked[0],
        stacked[1],
        stacked[2],
        stacked[3],
        stacked[4],
        stacked[5],
        stacked[6],
        stacked[7],
    )


def solution(mesh):
    return jax.shard_map(
        shards,
        mesh=mesh,
        in_specs=(
            P(("replica", "fsdp"), "seq", None),
            P(("replica", "fsdp"), "seq", None),
            P(None, "fsdp", None),
            P(None, "fsdp", None),
            P(None, "fsdp", None),
            P(None, "fsdp", None),
            P(None, None, "fsdp"),
            P(None, "fsdp"),
            P(None, "fsdp"),
            P(None, "fsdp"),
            P(("replica", "fsdp")),
            P(("replica", "fsdp"), None),
            P(("replica", "fsdp")),
        ),
        out_specs=(
            P(("replica", "fsdp"), "seq", None),
            P(("replica", "fsdp"), "seq", None),
            P(None, "fsdp", None),
            P(None, "fsdp", None),
            P(None, "fsdp", None),
            P(None, "fsdp", None),
            P(None, None, "fsdp"),
            P(None, "fsdp"),
            P(None, "fsdp"),
            P(None, "fsdp"),
        ),
        check_vma=False,
    )
```

profile of v0, /device:TPU:0, one launch (start us, length us, event | category | flops | bytes accessed | tf_op | source)
XLA Modules:
  0.0 1406.5 jit_solution(13420251808383852536)
XLA Ops:
  10.7 17.4 %all-gather = bf16[1,2,1280]{1,0,2:T(2,128)(2,1)S(1)} all-gather(bf16[1,2,160]{1,0,2:T(2,128)(2,1)S(1)} %copy.71), channel_id=2, replica_groups=mesh['replica'=2,'fsdp'=8,'seq'=2] {'fsdp'}, dimensions={2}, use_global_device_ids=true | all-gather | bytes 5760 | tf_op jit(solution)/shard_map/all_gather | solution.py:262
  28.9 20.9 %fusion.139 = (f32[1280]{0:T(1024)S(1)}, f32[1280]{0:T(1024)S(1)}) fusion(bf16[1,2,1280]{1,0,2:T(2,128)(2,1)S(1)} %all-gather), kind=kLoop, calls=%fused_computation.149 | loop fusion | flops 2560 | bytes 15360 | tf_op jit(solution)/shard_map/mul | solution.py:38
  49.9 58.0 %all-gather.31.cloned.1.call-done = bf16[1,1280,3840]{2,1,0:T(8,128)(2,1)} async-done(((bf16[1,160,3840]{2,1,0:T(8,128)(2,1)}), bf16[1,1280,3840]{2,1,0:T(8,128)(2,1)}) %all-gather.31.cloned.1.call-update) | async-done | bytes 9830416 | tf_op jit(solution)/shard_map/all_gather | solution.py:258
  131.1 26.5 %all-reduce.13 = (bf16[80]{0:T(256)(128)(2,1)S(1)}, bf16[1280]{0:T(1024)(128)(2,1)S(1)}, bf16[1280]{0:T(1024)(128)(2,1)S(1)}, bf16[80]{0:T(256)(128)(2,1)S(1)}, bf16[1280]{0:T(1024)(128)(2,1)S(1)}) all-reduce(bf16[80]{0:T(256)(128)(2,1)S(1)} %dynamic-update-slice, ...), channel_id=4, replica_groups=mesh['replica'=2,'fsdp'=8,'seq'=2] {'fsdp'}, use_global_device_ids=true, to_apply=%add | all-reduce | flops 4000 | bytes 16000
  179.8 21.0 %fusion.137 = (f32[1280]{0:T(1024)S(1)}, f32[1280]{0:T(1024)S(1)}) fusion(bf16[1,2,1280]{1,0,2:T(2,128)(2,1)S(1)} %all-gather.8), kind=kLoop, calls=%fused_computation.145 | loop fusion | flops 2560 | bytes 15360 | tf_op jit(solution)/shard_map/mul | solution.py:38
  243.2 35.7 %all-gather.37.cloned.1.call-done = bf16[1,1280,1280]{2,1,0:T(8,128)(2,1)} async-done(((bf16[1,160,1280]{2,1,0:T(8,128)(2,1)}), bf16[1,1280,1280]{2,1,0:T(8,128)(2,1)}) %all-gather.37.cloned.1.call-update) | async-done | bytes 3276816 | tf_op jit(solution)/shard_map/all_gather | solution.py:261
  282.9 90.4 %all-gather.39.cloned.1.call-done = bf16[1,1280,3840]{2,1,0:T(8,128)(2,1)} async-done(((bf16[1,160,3840]{2,1,0:T(8,128)(2,1)}), bf16[1,1280,3840]{2,1,0:T(8,128)(2,1)}) %all-gather.39.cloned.1.call-update) | async-done | bytes 9830416 | tf_op jit(solution)/shard_map/all_gather | solution.py:258
  389.5 31.1 %all-gather.29.cloned.1.call-done = bf16[1,2560,512]{1,2,0:T(8,128)(2,1)} async-done(((bf16[1,2560,256]{1,2,0:T(8,128)(2,1)}), bf16[1,2560,512]{1,2,0:T(8,128)(2,1)}) %all-gather.29.cloned.1.call-update) | async-done | bytes 2621456 | tf_op jit(solution)/shard_map/all_gather | solution.py:68
  439.0 22.6 %all-gather.41.cloned.1.call-done = bf16[1,1280,1280]{2,1,0:T(8,128)(2,1)} async-done(((bf16[1,160,1280]{2,1,0:T(8,128)(2,1)}), bf16[1,1280,1280]{2,1,0:T(8,128)(2,1)}) %all-gather.41.cloned.1.call-update) | async-done | bytes 3276816 | tf_op jit(solution)/shard_map/all_gather | solution.py:259
  466.3 35.2 %all-gather.43.cloned.1.call-done = bf16[1,1280,1280]{2,1,0:T(8,128)(2,1)} async-done(((bf16[1,160,1280]{2,1,0:T(8,128)(2,1)}), bf16[1,1280,1280]{2,1,0:T(8,128)(2,1)}) %all-gather.43.cloned.1.call-update) | async-done | bytes 3276816 | tf_op jit(solution)/shard_map/all_gather | solution.py:260
  506.1 35.2 %all-gather.45.cloned.1.call-done = bf16[1,1280,1280]{2,1,0:T(8,128)(2,1)} async-done(((bf16[1,160,1280]{2,1,0:T(8,128)(2,1)}), bf16[1,1280,1280]{2,1,0:T(8,128)(2,1)}) %all-gather.45.cloned.1.call-update) | async-done | bytes 3276816 | tf_op jit(solution)/shard_map/all_gather | solution.py:261
  598.7 37.6 %reduce-scatter.19.cloned.1.call-done = f32[1,1280,256]{2,1,0:T(8,128)} async-done(((f32[1,1280,512]{2,1,0:T(8,128)}), f32[1,1280,256]{2,1,0:T(8,128)}) %reduce-scatter.19.cloned.1.call-update) | async-done | bytes 1310736 | tf_op jit(solution)/shard_map/reduce_scatter | solution.py:181
  722.4 20.2 %reduce-scatter.23.cloned.1.call-done = f32[1,1280,256]{2,1,0:T(8,128)} async-done(((f32[1,1280,512]{2,1,0:T(8,128)}), f32[1,1280,256]{2,1,0:T(8,128)}) %reduce-scatter.23.cloned.1.call-update) | async-done | bytes 1310736 | tf_op jit(solution)/shard_map/reduce_scatter | solution.py:181
  760.5 25.6 %reduce-scatter.37.cloned.1.call-done = bf16[160,1280]{1,0:T(8,128)(2,1)} async-done(((bf16[1280,1280]{1,0:T(8,128)(2,1)}), bf16[160,1280]{1,0:T(8,128)(2,1)}) %reduce-scatter.37.cloned.1.call-update) | async-done | bytes 409616 | tf_op jit(solution)/shard_map/reduce_scatter | solution.py:302
  786.1 42.4 %reduce-scatter.33.cloned.1.call-done = bf16[160,1280]{1,0:T(8,128)(2,1)} async-done(((bf16[1280,1280]{1,0:T(8,128)(2,1)}), bf16[160,1280]{1,0:T(8,128)(2,1)}) %reduce-scatter.33.cloned.1.call-update) | async-done | bytes 409616 | tf_op jit(solution)/shard_map/reduce_scatter | solution.py:299
  828.6 42.4 %reduce-scatter.41.cloned.1.call-done = bf16[160,1280]{1,0:T(8,128)(2,1)} async-done(((bf16[1280,1280]{1,0:T(8,128)(2,1)}), bf16[160,1280]{1,0:T(8,128)(2,1)}) %reduce-scatter.41.cloned.1.call-update) | async-done | bytes 409616 | tf_op jit(solution)/shard_map/reduce_scatter | solution.py:305
  870.9 42.4 %reduce-scatter.39.cloned.1.call-done = bf16[160,1280]{1,0:T(8,128)(2,1)} async-done(((bf16[1280,1280]{1,0:T(8,128)(2,1)}), bf16[160,1280]{1,0:T(8,128)(2,1)}) %reduce-scatter.39.cloned.1.call-update) | async-done | bytes 409616 | tf_op jit(solution)/shard_map/reduce_scatter | solution.py:305
  913.4 42.5 %reduce-scatter.35.cloned.1.call-done = bf16[160,1280]{1,0:T(8,128)(2,1)} async-done(((bf16[1280,1280]{1,0:T(8,128)(2,1)}), bf16[160,1280]{1,0:T(8,128)(2,1)}) %reduce-scatter.35.cloned.1.call-update) | async-done | bytes 409616 | tf_op jit(solution)/shard_map/reduce_scatter | solution.py:302
  955.9 42.4 %reduce-scatter.31.cloned.1.call-done = bf16[160,1280]{1,0:T(8,128)(2,1)} async-done(((bf16[1280,1280]{1,0:T(8,128)(2,1)}), bf16[160,1280]{1,0:T(8,128)(2,1)}) %reduce-scatter.31.cloned.1.call-update) | async-done | bytes 409616 | tf_op jit(solution)/shard_map/reduce_scatter | solution.py:299
  998.3 104.4 %reduce-scatter.29.cloned.1.call-done = bf16[160,3840]{1,0:T(8,128)(2,1)} async-done(((bf16[1280,3840]{1,0:T(8,128)(2,1)}), bf16[160,3840]{1,0:T(8,128)(2,1)}) %reduce-scatter.29.cloned.1.call-update) | async-done | bytes 1228816 | tf_op jit(solution)/shard_map/reduce_scatter | solution.py:296
  1102.7 104.0 %reduce-scatter.27.cloned.1.call-done = bf16[160,3840]{1,0:T(8,128)(2,1)} async-done(((bf16[1280,3840]{1,0:T(8,128)(2,1)}), bf16[160,3840]{1,0:T(8,128)(2,1)}) %reduce-scatter.27.cloned.1.call-update) | async-done | bytes 1228816 | tf_op jit(solution)/shard_map/reduce_scatter | solution.py:296
  1208.5 26.4 %all-reduce.12 = (bf16[1280]{0:T(1024)(128)(2,1)S(1)}, bf16[1280]{0:T(1024)(128)(2,1)S(1)}, bf16[1280]{0:T(1024)(128)(2,1)S(1)}, bf16[1280]{0:T(1024)(128)(2,1)S...) all-reduce(bf16[1280]{0:T(1024)(128)(2,1)S(1)} %dynamic-update-slic, ...), channel_id=17, replica_groups=mesh['replica'=2,'fsdp'=8,'seq'=2] {'fsdp'}, use_global_device_ids=true, to_apply=%add.5 | all-reduce | flops 6560 | bytes 26240
  1243.3 26.8 %reduce-scatter.43.cloned.1.call-done = bf16[160,2]{1,0:T(8,128)(2,1)} async-done(((bf16[1280,2]{1,0:T(8,128)(2,1)}), bf16[160,2]{1,0:T(8,128)(2,1)}) %reduce-scatter.43.cloned.1.call-update) | async-done | bytes 656
  1283.2 107.7 %all-reduce.18.cloned.1.call-done = (bf16[1,160,3840]{2,1,0:T(8,128)(2,1)}, bf16[1,160,3840]{2,1,0:T(8,128)(2,1)}, bf16[1,160,1280]{2,1,0:T(8,128)(2,1)}, bf16[1...) async-done(((bf16[1,160,3840]{2,1,0:T(8,128)(2,1)}, ...) | async-done | bytes 4915216 | tf_op jit(solution)/shard_map/psum | solution.py:322
  (319 shorter events, 325.7 us)
Async XLA Ops:
  7.2 100.7 %all-gather.31.cloned.1.call-start = ((), (), s32[]{:S(2)}) async-start(), calls=%async_computation.28 | async-start | bytes 11059200 | tf_op jit(solution)/shard_map/all_gather | solution.py:258
  10.5 192.0 %all-gather.27.cloned.1.call-start = ((), (), s32[]{:S(2)}) async-start(), calls=%async_computation.14 | async-start | bytes 3932160 | tf_op jit(solution)/shard_map/all_gather | solution.py:68
  117.7 113.2 %all-gather.33.cloned.1.call-start = ((), (), s32[]{:S(2)}) async-start(), calls=%async_computation.29 | async-start | bytes 3686400 | tf_op jit(solution)/shard_map/all_gather | solution.py:259
  119.8 119.4 %all-gather.35.cloned.1.call-start = ((), (), s32[]{:S(2)}) async-start(), calls=%async_computation.30 | async-start | bytes 3686400 | tf_op jit(solution)/shard_map/all_gather | solution.py:260
  120.8 158.1 %all-gather.37.cloned.1.call-start = ((), (), s32[]{:S(2)}) async-start(), calls=%async_computation.31 | async-start | bytes 3686400 | tf_op jit(solution)/shard_map/all_gather | solution.py:261
  122.1 251.2 %all-gather.39.cloned.1.call-start = ((), (), s32[]{:S(2)}) async-start(), calls=%async_computation.32 | async-start | bytes 11059200 | tf_op jit(solution)/shard_map/all_gather | solution.py:258
  122.6 297.9 %all-gather.29.cloned.1.call-start = ((), (), s32[]{:S(2)}) async-start(), calls=%async_computation.15 | async-start | bytes 3932160 | tf_op jit(solution)/shard_map/all_gather | solution.py:68
  383.0 78.6 %all-gather.41.cloned.1.call-start = ((), (), s32[]{:S(2)}) async-start(), calls=%async_computation.33 | async-start | bytes 3686400 | tf_op jit(solution)/shard_map/all_gather | solution.py:259
  383.7 117.8 %all-gather.43.cloned.1.call-start = ((), (), s32[]{:S(2)}) async-start(), calls=%async_computation.34 | async-start | bytes 3686400 | tf_op jit(solution)/shard_map/all_gather | solution.py:260
  384.5 156.8 %all-gather.45.cloned.1.call-start = ((), (), s32[]{:S(2)}) async-start(), calls=%async_computation.35 | async-start | bytes 3686400 | tf_op jit(solution)/shard_map/all_gather | solution.py:261
  385.1 211.4 %reduce-scatter.21.cloned.1.call-start = ((), (), s32[]{:S(2)}) async-start(), calls=%async_computation.17 | async-start | bytes 3932160 | tf_op jit(solution)/shard_map/reduce_scatter | solution.py:187
  575.0 145.9 %reduce-scatter.25.cloned.1.call-start = ((), (), s32[]{:S(2)}) async-start(), calls=%async_computation.19 | async-start | bytes 3932160 | tf_op jit(solution)/shard_map/reduce_scatter | solution.py:187
  665.1 77.5 %reduce-scatter.23.cloned.1.call-start = ((), (), s32[]{:S(2)}) async-start(), calls=%async_computation.18 | async-start | bytes 3932160 | tf_op jit(solution)/shard_map/reduce_scatter | solution.py:181
  679.9 106.2 %reduce-scatter.37.cloned.1.call-start = ((), (), s32[]{:S(2)}) async-start(), calls=%async_computation.25 | async-start | bytes 3686400 | tf_op jit(solution)/shard_map/reduce_scatter | solution.py:302
  684.3 144.3 %reduce-scatter.33.cloned.1.call-start = ((), (), s32[]{:S(2)}) async-start(), calls=%async_computation.23 | async-start | bytes 3686400 | tf_op jit(solution)/shard_map/reduce_scatter | solution.py:299
  688.6 182.4 %reduce-scatter.41.cloned.1.call-start = ((), (), s32[]{:S(2)}) async-start(), calls=%async_computation.27 | async-start | bytes 3686400 | tf_op jit(solution)/shard_map/reduce_scatter | solution.py:305
  693.1 220.2 %reduce-scatter.39.cloned.1.call-start = ((), (), s32[]{:S(2)}) async-start(), calls=%async_computation.26 | async-start | bytes 3686400 | tf_op jit(solution)/shard_map/reduce_scatter | solution.py:305
  698.0 257.9 %reduce-scatter.35.cloned.1.call-start = ((), (), s32[]{:S(2)}) async-start(), calls=%async_computation.24 | async-start | bytes 3686400 | tf_op jit(solution)/shard_map/reduce_scatter | solution.py:302
  702.3 296.0 %reduce-scatter.31.cloned.1.call-start = ((), (), s32[]{:S(2)}) async-start(), calls=%async_computation.22 | async-start | bytes 3686400 | tf_op jit(solution)/shard_map/reduce_scatter | solution.py:299
  706.7 396.0 %reduce-scatter.29.cloned.1.call-start = ((), (), s32[]{:S(2)}) async-start(), calls=%async_computation.21 | async-start | bytes 11059200 | tf_op jit(solution)/shard_map/reduce_scatter | solution.py:296
  715.1 491.7 %reduce-scatter.27.cloned.1.call-start = ((), (), s32[]{:S(2)}) async-start(), calls=%async_computation.20 | async-start | bytes 11059200 | tf_op jit(solution)/shard_map/reduce_scatter | solution.py:296
  750.7 489.2 %reduce-scatter.45.cloned.1.call-start = ((), (), s32[]{:S(2)}) async-start(), calls=%async_computation.37 | async-start | bytes 368640
  751.7 518.3 %reduce-scatter.43.cloned.1.call-start = ((), (), s32[]{:S(2)}) async-start(), calls=%async_computation.36 | async-start | bytes 368640
  760.5 630.4 %all-reduce.18.cloned.1.call-start = ((), (), s32[]{:S(2)}) async-start(), calls=%async_computation.38 | async-start | bytes 9830400 | tf_op jit(solution)/shard_map/psum | solution.py:322
  (62 other events, 678.4 us)
Sparse Core Ops, SparseCore 0:
  10.6 97.2 all-gather.30
  117.8 37.5 all-gather.26
  157.6 40.0 all-gather.32
  199.8 39.3 all-gather.34
  240.6 38.2 all-gather.36
  280.4 92.8 all-gather.38
  383.1 37.4 all-gather.28
  422.2 39.3 all-gather.40
  463.3 38.2 all-gather.42
  503.0 38.2 all-gather.44
  560.0 36.4 reduce-scatter.20
  598.6 37.5 reduce-scatter.18
  665.2 37.5 reduce-scatter.24
  704.9 37.5 reduce-scatter.22
  744.7 41.3 reduce-scatter.36
  788.4 40.1 reduce-scatter.32
  830.7 40.1 reduce-scatter.40
  873.2 40.1 reduce-scatter.38
  915.7 40.1 reduce-scatter.34
  958.1 40.1 reduce-scatter.30
  1000.6 102.0 reduce-scatter.28
  1105.1 101.5 reduce-scatter.26
  1209.6 28.8 reduce-scatter.44
  1274.5 116.3 all-reduce.17
  (1 shorter events, 28.6 us)
where the time goes:
time: 1420 us; the launch traced here: 1410 us
  waiting for transfers between devices  971 us (68%)
  matrix products  173 us (12%)
  blocking collectives  96.6 us (7%)
  other arithmetic  82.8 us (6%)
  local copies, waits for them, and re-layouts  59.5 us (4%)
  between operations  21.9 us (2%)
    reduce_scatter x2, waiting for transfers between devices, shards(): lax.psum_scatter(layer_grads[0].astype(jnp.bfloat16), 'fsdp', scatter_dim...  208 us
    all_gather x2, waiting for transfers between devices, shards(): lax.all_gather(qkv_weight[layer_index], 'fsdp', axis=0, tiled=True)  148 us
    psum x1, waiting for transfers between devices, shards(): lax.psum(shares[0].astype(jnp.bfloat16), ('replica', 'seq'))  108 us
    reduce_scatter x2, waiting for transfers between devices, shards(): lax.psum_scatter(layer_grads[1].astype(jnp.bfloat16), 'fsdp', scatter_dim...  84.9 us
    reduce_scatter x2, waiting for transfers between devices, shards(): lax.psum_scatter(layer_grads[3].astype(jnp.bfloat16), 'fsdp', scatter_dim...  84.8 us
    all_gather x2, waiting for transfers between devices, shards(): lax.all_gather(down_weight[layer_index], 'fsdp', axis=0, tiled=True)  70.9 us
    reduce_scatter x2, waiting for transfers between devices, shards(): lax.psum_scatter(layer_grads[2].astype(jnp.bfloat16), 'fsdp', scatter_dim...  68.1 us
    reduce_scatter x2, waiting for transfers between devices, backward_layer(): lax.psum_scatter(key_grad.reshape(series_count, model_width, total_length...  57.8 us
  transfers between devices with their start and end apart: 25, of which 21 were waited for; matrix products, arithmetic and copies ran while one was open for 16% of the time, Pallas kernels for 0%

commit v1 on v0

--- a/solution.py
+++ b/solution.py
@@ -319,7 +319,9 @@
             ).astype(jnp.float32),
         )
         shares = (
-            lax.psum(shares[0].astype(jnp.bfloat16), ("replica", "seq")).astype(jnp.float32),
+            lax.psum(lax.psum(shares[0].astype(jnp.bfloat16), "seq"), "replica").astype(
+                jnp.float32
+            ),
             lax.psum(shares[1].astype(jnp.bfloat16), ("replica", "seq")).astype(jnp.float32),
             lax.psum(shares[2].astype(jnp.bfloat16), ("replica", "seq")).astype(jnp.float32),
             lax.psum(shares[3].astype(jnp.bfloat16), ("replica", "seq")).astype(jnp.float32),

time: 1420 us -> 1520 us (1.070)
  waiting for transfers between devices: 971 us -> 1060 us
    psum x1 -> x3, waiting for transfers between devices: 108 us -> 175 us  [the longest x1 68.1 us: shards(): lax.psum(lax.psum(shares[0].astype(jnp.bfloat16), 'seq'), 'replica')]
    reduce_scatter x2, waiting for transfers between devices: 208 us -> 170 us  [shards(): lax.psum_scatter(layer_grads[0].astype(jnp.bfloat16), 'fsdp', scatter_dim...]
    unnamed x27 -> x29, waiting for transfers between devices: 29.5 us -> 59.4 us
    reduce_scatter x2, waiting for transfers between devices: 57.8 us -> 76 us  [backward_layer(): lax.psum_scatter(key_grad.reshape(series_count, model_width, total_length...]
  transfers between devices with their start and end apart: 25 -> 27, of which waited for: 21 -> 25; matrix products, arithmetic and copies ran while one was open for 16% -> 16% of each run, Pallas kernels for 0% -> 0%
where the time goes in v1:
time: 1520 us; the launch traced here: 1510 us
  waiting for transfers between devices  1060 us (70%)
  matrix products  170 us (11%)
  blocking collectives  97.7 us (6%)
  other arithmetic  87.3 us (6%)
  local copies, waits for them, and re-layouts  66.3 us (4%)
  between operations  22.2 us (1%)
    reduce_scatter x2, waiting for transfers between devices, shards(): lax.psum_scatter(layer_grads[0].astype(jnp.bfloat16), 'fsdp', scatter_dim...  170 us
    all_gather x2, waiting for transfers between devices, shards(): lax.all_gather(qkv_weight[layer_index], 'fsdp', axis=0, tiled=True)  148 us
    reduce_scatter x2, waiting for transfers between devices, shards(): lax.psum_scatter(layer_grads[1].astype(jnp.bfloat16), 'fsdp', scatter_dim...  85.7 us
    reduce_scatter x2, waiting for transfers between devices, shards(): lax.psum_scatter(layer_grads[3].astype(jnp.bfloat16), 'fsdp', scatter_dim...  85 us
    reduce_scatter x2, waiting for transfers between devices, backward_layer(): lax.psum_scatter(key_grad.reshape(series_count, model_width, total_length...  76 us
    reduce_scatter x2, waiting for transfers between devices, shards(): lax.psum_scatter(layer_grads[2].astype(jnp.bfloat16), 'fsdp', scatter_dim...  73.9 us
    all_gather x2, waiting for transfers between devices, shards(): lax.all_gather(down_weight[layer_index], 'fsdp', axis=0, tiled=True)  71 us
    psum x1, waiting for transfers between devices, shards(): lax.psum(lax.psum(shares[0].astype(jnp.bfloat16), 'seq'), 'replica')  68.1 us
  transfers between devices with their start and end apart: 27, of which 25 were waited for; matrix products, arithmetic and copies ran while one was open for 16% of the time, Pallas kernels for 0%

profile of v1, /device:TPU:0, one launch (start us, length us, event | category | flops | bytes accessed | tf_op | source)
XLA Modules:
  0.0 1507.5 jit_solution(12112051656863880916)
XLA Ops:
  49.9 58.0 %all-gather.31.cloned.1.call-done = bf16[1,1280,3840]{2,1,0:T(8,128)(2,1)} async-done(((bf16[1,160,3840]{2,1,0:T(8,128)(2,1)}), bf16[1,1280,3840]{2,1,0:T(8,128)(2,1)}) %all-gather.31.cloned.1.call-update) | async-done | bytes 9830416 | tf_op jit(solution)/shard_map/all_gather | solution.py:258
  131.1 26.5 %all-reduce.13 = (bf16[80]{0:T(256)(128)(2,1)S(1)}, bf16[1280]{0:T(1024)(128)(2,1)S(1)}, bf16[1280]{0:T(1024)(128)(2,1)S(1)}, bf16[80]{0:T(256)(128)(2,1)S(1)}, bf16[1280]{0:T(1024)(128)(2,1)S(1)}) all-reduce(bf16[80]{0:T(256)(128)(2,1)S(1)} %dynamic-update-slice, ...), channel_id=4, replica_groups=mesh['replica'=2,'fsdp'=8,'seq'=2] {'fsdp'}, use_global_device_ids=true, to_apply=%add | all-reduce | flops 4000 | bytes 16000
  243.2 35.7 %all-gather.37.cloned.1.call-done = bf16[1,1280,1280]{2,1,0:T(8,128)(2,1)} async-done(((bf16[1,160,1280]{2,1,0:T(8,128)(2,1)}), bf16[1,1280,1280]{2,1,0:T(8,128)(2,1)}) %all-gather.37.cloned.1.call-update) | async-done | bytes 3276816 | tf_op jit(solution)/shard_map/all_gather | solution.py:261
  283.5 89.8 %all-gather.39.cloned.1.call-done = bf16[1,1280,3840]{2,1,0:T(8,128)(2,1)} async-done(((bf16[1,160,3840]{2,1,0:T(8,128)(2,1)}), bf16[1,1280,3840]{2,1,0:T(8,128)(2,1)}) %all-gather.39.cloned.1.call-update) | async-done | bytes 9830416 | tf_op jit(solution)/shard_map/all_gather | solution.py:258
  389.4 31.1 %all-gather.29.cloned.1.call-done = bf16[1,2560,512]{1,2,0:T(8,128)(2,1)} async-done(((bf16[1,2560,256]{1,2,0:T(8,128)(2,1)}), bf16[1,2560,512]{1,2,0:T(8,128)(2,1)}) %all-gather.29.cloned.1.call-update) | async-done | bytes 2621456 | tf_op jit(solution)/shard_map/all_gather | solution.py:68
  439.0 22.6 %all-gather.41.cloned.1.call-done = bf16[1,1280,1280]{2,1,0:T(8,128)(2,1)} async-done(((bf16[1,160,1280]{2,1,0:T(8,128)(2,1)}), bf16[1,1280,1280]{2,1,0:T(8,128)(2,1)}) %all-gather.41.cloned.1.call-update) | async-done | bytes 3276816 | tf_op jit(solution)/shard_map/all_gather | solution.py:259
  466.8 34.7 %all-gather.43.cloned.1.call-done = bf16[1,1280,1280]{2,1,0:T(8,128)(2,1)} async-done(((bf16[1,160,1280]{2,1,0:T(8,128)(2,1)}), bf16[1,1280,1280]{2,1,0:T(8,128)(2,1)}) %all-gather.43.cloned.1.call-update) | async-done | bytes 3276816 | tf_op jit(solution)/shard_map/all_gather | solution.py:260
  506.0 35.3 %all-gather.45.cloned.1.call-done = bf16[1,1280,1280]{2,1,0:T(8,128)(2,1)} async-done(((bf16[1,160,1280]{2,1,0:T(8,128)(2,1)}), bf16[1,1280,1280]{2,1,0:T(8,128)(2,1)}) %all-gather.45.cloned.1.call-update) | async-done | bytes 3276816 | tf_op jit(solution)/shard_map/all_gather | solution.py:261
  598.6 37.6 %reduce-scatter.19.cloned.1.call-done = f32[1,1280,256]{2,1,0:T(8,128)} async-done(((f32[1,1280,512]{2,1,0:T(8,128)}), f32[1,1280,256]{2,1,0:T(8,128)}) %reduce-scatter.19.cloned.1.call-update) | async-done | bytes 1310736 | tf_op jit(solution)/shard_map/reduce_scatter | solution.py:181
  704.2 38.4 %reduce-scatter.23.cloned.1.call-done = f32[1,1280,256]{2,1,0:T(8,128)} async-done(((f32[1,1280,512]{2,1,0:T(8,128)}), f32[1,1280,256]{2,1,0:T(8,128)}) %reduce-scatter.23.cloned.1.call-update) | async-done | bytes 1310736 | tf_op jit(solution)/shard_map/reduce_scatter | solution.py:181
  782.2 65.9 %reduce-scatter.29.cloned.1.call-done = bf16[160,3840]{1,0:T(8,128)(2,1)} async-done(((bf16[1280,3840]{1,0:T(8,128)(2,1)}), bf16[160,3840]{1,0:T(8,128)(2,1)}) %reduce-scatter.29.cloned.1.call-update) | async-done | bytes 1228816 | tf_op jit(solution)/shard_map/reduce_scatter | solution.py:296
  848.0 103.9 %reduce-scatter.27.cloned.1.call-done = bf16[160,3840]{1,0:T(8,128)(2,1)} async-done(((bf16[1280,3840]{1,0:T(8,128)(2,1)}), bf16[160,3840]{1,0:T(8,128)(2,1)}) %reduce-scatter.27.cloned.1.call-update) | async-done | bytes 1228816 | tf_op jit(solution)/shard_map/reduce_scatter | solution.py:296
  962.4 31.4 %reduce-scatter.37.cloned.1.call-done = bf16[160,1280]{1,0:T(8,128)(2,1)} async-done(((bf16[1280,1280]{1,0:T(8,128)(2,1)}), bf16[160,1280]{1,0:T(8,128)(2,1)}) %reduce-scatter.37.cloned.1.call-update) | async-done | bytes 409616 | tf_op jit(solution)/shard_map/reduce_scatter | solution.py:302
  993.8 43.0 %reduce-scatter.33.cloned.1.call-done = bf16[160,1280]{1,0:T(8,128)(2,1)} async-done(((bf16[1280,1280]{1,0:T(8,128)(2,1)}), bf16[160,1280]{1,0:T(8,128)(2,1)}) %reduce-scatter.33.cloned.1.call-update) | async-done | bytes 409616 | tf_op jit(solution)/shard_map/reduce_scatter | solution.py:299
  1036.9 42.5 %reduce-scatter.41.cloned.1.call-done = bf16[160,1280]{1,0:T(8,128)(2,1)} async-done(((bf16[1280,1280]{1,0:T(8,128)(2,1)}), bf16[160,1280]{1,0:T(8,128)(2,1)}) %reduce-scatter.41.cloned.1.call-update) | async-done | bytes 409616 | tf_op jit(solution)/shard_map/reduce_scatter | solution.py:305
  1079.4 42.5 %reduce-scatter.39.cloned.1.call-done = bf16[160,1280]{1,0:T(8,128)(2,1)} async-done(((bf16[1280,1280]{1,0:T(8,128)(2,1)}), bf16[160,1280]{1,0:T(8,128)(2,1)}) %reduce-scatter.39.cloned.1.call-update) | async-done | bytes 409616 | tf_op jit(solution)/shard_map/reduce_scatter | solution.py:305
  1121.8 42.5 %reduce-scatter.35.cloned.1.call-done = bf16[160,1280]{1,0:T(8,128)(2,1)} async-done(((bf16[1280,1280]{1,0:T(8,128)(2,1)}), bf16[160,1280]{1,0:T(8,128)(2,1)}) %reduce-scatter.35.cloned.1.call-update) | async-done | bytes 409616 | tf_op jit(solution)/shard_map/reduce_scatter | solution.py:302
  1164.4 42.6 %reduce-scatter.31.cloned.1.call-done = bf16[160,1280]{1,0:T(8,128)(2,1)} async-done(((bf16[1280,1280]{1,0:T(8,128)(2,1)}), bf16[160,1280]{1,0:T(8,128)(2,1)}) %reduce-scatter.31.cloned.1.call-update) | async-done | bytes 409616 | tf_op jit(solution)/shard_map/reduce_scatter | solution.py:299
  1209.8 27.4 %all-reduce.12 = (bf16[1280]{0:T(1024)(128)(2,1)S(1)}, bf16[1280]{0:T(1024)(128)(2,1)S(1)}, bf16[1280]{0:T(1024)(128)(2,1)S(1)}, bf16[1280]{0:T(1024)(128)(2,1)S...) all-reduce(bf16[1280]{0:T(1024)(128)(2,1)S(1)} %dynamic-update-slic, ...), channel_id=17, replica_groups=mesh['replica'=2,'fsdp'=8,'seq'=2] {'fsdp'}, use_global_device_ids=true, to_apply=%add.5 | all-reduce | flops 6560 | bytes 26240
  1237.2 42.0 %all-reduce.24.cloned.1.call-done = (bf16[160,3840]{1,0:T(8,128)(2,1)}, bf16[160,3840]{1,0:T(8,128)(2,1)}) async-done(((bf16[160,3840]{1,0:T(8,128)(2,1)}, bf16[160,3840]{1,0:T(8,128)(2,1)}), (bf16[160,3840]{1,0:T(8,128)(2,1)}, bf16[160,3840]{1,0:T(8,128)(2,1)})) %all-reduce.24.cloned.1.call-update) | async-done | bytes 2457616 | tf_op jit(solution)/shard_map/psum | solution.py:322
  1284.0 28.3 %reduce-scatter.45.cloned.1.call-done = bf16[160,2]{1,0:T(8,128)(2,1)} async-done(((bf16[1280,2]{1,0:T(8,128)(2,1)}), bf16[160,2]{1,0:T(8,128)(2,1)}) %reduce-scatter.45.cloned.1.call-update) | async-done | bytes 656
  1315.8 28.2 %reduce-scatter.43.cloned.1.call-done = bf16[160,2]{1,0:T(8,128)(2,1)} async-done(((bf16[1280,2]{1,0:T(8,128)(2,1)}), bf16[160,2]{1,0:T(8,128)(2,1)}) %reduce-scatter.43.cloned.1.call-update) | async-done | bytes 656
  1357.3 65.5 %all-reduce.22.cloned.1.call-done = (bf16[1,160,1280]{2,1,0:T(8,128)(2,1)}, bf16[1,160,1280]{2,1,0:T(8,128)(2,1)}, bf16[1,160,1280]{2,1,0:T(8,128)(2,1)}, bf16[1...) async-done(((bf16[1,160,1280]{2,1,0:T(8,128)(2,1)}, bf16[1,160,1280]{2,1,0:T(8,128)(2,1)}, bf16[1,160,1280]{2,1,0:T(8,128)(2,1)}, ...) | async-done | bytes 2457616 | tf_op jit(solution)/shard_map/psum | solution.py:325
  1427.9 68.1 %all-reduce.26.cloned.1.call-done = (bf16[1,160,3840]{2,1,0:T(8,128)(2,1)}, bf16[1,160,3840]{2,1,0:T(8,128)(2,1)}) async-done(((bf16[1,160,3840]{2,1,0:T(8,128)(2,1)}, bf16[1,160,3840]{2,1,0:T(8,128)(2,1)}), (bf16[1,160,3840]{2,1,0:T(8,128)(2,1)}, bf16[1,160,3840]{2,1,0:T(8,128)(2,1)})) %all-reduce.26.cloned.1.call-update) | async-done | bytes 2457616 | tf_op jit(solution)/shard_map/psum | solution.py:322
  (331 shorter events, 401.9 us)
Async XLA Ops:
  7.2 100.7 %all-gather.31.cloned.1.call-start = ((), (), s32[]{:S(2)}) async-start(), calls=%async_computation.28 | async-start | bytes 11059200 | tf_op jit(solution)/shard_map/all_gather | solution.py:258
  10.5 192.0 %all-gather.27.cloned.1.call-start = ((), (), s32[]{:S(2)}) async-start(), calls=%async_computation.14 | async-start | bytes 3932160 | tf_op jit(solution)/shard_map/all_gather | solution.py:68
  117.7 113.2 %all-gather.33.cloned.1.call-start = ((), (), s32[]{:S(2)}) async-start(), calls=%async_computation.29 | async-start | bytes 3686400 | tf_op jit(solution)/shard_map/all_gather | solution.py:259
  119.7 119.4 %all-gather.35.cloned.1.call-start = ((), (), s32[]{:S(2)}) async-start(), calls=%async_computation.30 | async-start | bytes 3686400 | tf_op jit(solution)/shard_map/all_gather | solution.py:260
  120.8 158.1 %all-gather.37.cloned.1.call-start = ((), (), s32[]{:S(2)}) async-start(), calls=%async_computation.31 | async-start | bytes 3686400 | tf_op jit(solution)/shard_map/all_gather | solution.py:261
  122.0 251.2 %all-gather.39.cloned.1.call-start = ((), (), s32[]{:S(2)}) async-start(), calls=%async_computation.32 | async-start | bytes 11059200 | tf_op jit(solution)/shard_map/all_gather | solution.py:258
  122.6 297.9 %all-gather.29.cloned.1.call-start = ((), (), s32[]{:S(2)}) async-start(), calls=%async_computation.15 | async-start | bytes 3932160 | tf_op jit(solution)/shard_map/all_gather | solution.py:68
  383.7 117.8 %all-gather.43.cloned.1.call-start = ((), (), s32[]{:S(2)}) async-start(), calls=%async_computation.34 | async-start | bytes 3686400 | tf_op jit(solution)/shard_map/all_gather | solution.py:260
  384.5 156.8 %all-gather.45.cloned.1.call-start = ((), (), s32[]{:S(2)}) async-start(), calls=%async_computation.35 | async-start | bytes 3686400 | tf_op jit(solution)/shard_map/all_gather | solution.py:261
  385.0 211.3 %reduce-scatter.21.cloned.1.call-start = ((), (), s32[]{:S(2)}) async-start(), calls=%async_computation.17 | async-start | bytes 3932160 | tf_op jit(solution)/shard_map/reduce_scatter | solution.py:187
  574.9 127.9 %reduce-scatter.25.cloned.1.call-start = ((), (), s32[]{:S(2)}) async-start(), calls=%async_computation.19 | async-start | bytes 3932160 | tf_op jit(solution)/shard_map/reduce_scatter | solution.py:187
  679.9 168.2 %reduce-scatter.29.cloned.1.call-start = ((), (), s32[]{:S(2)}) async-start(), calls=%async_computation.21 | async-start | bytes 11059200 | tf_op jit(solution)/shard_map/reduce_scatter | solution.py:296
  688.1 263.9 %reduce-scatter.27.cloned.1.call-start = ((), (), s32[]{:S(2)}) async-start(), calls=%async_computation.20 | async-start | bytes 11059200 | tf_op jit(solution)/shard_map/reduce_scatter | solution.py:296
  750.7 243.1 %reduce-scatter.37.cloned.1.call-start = ((), (), s32[]{:S(2)}) async-start(), calls=%async_computation.25 | async-start | bytes 3686400 | tf_op jit(solution)/shard_map/reduce_scatter | solution.py:302
  755.4 281.4 %reduce-scatter.33.cloned.1.call-start = ((), (), s32[]{:S(2)}) async-start(), calls=%async_computation.23 | async-start | bytes 3686400 | tf_op jit(solution)/shard_map/reduce_scatter | solution.py:299
  760.6 318.8 %reduce-scatter.41.cloned.1.call-start = ((), (), s32[]{:S(2)}) async-start(), calls=%async_computation.27 | async-start | bytes 3686400 | tf_op jit(solution)/shard_map/reduce_scatter | solution.py:305
  766.0 355.8 %reduce-scatter.39.cloned.1.call-start = ((), (), s32[]{:S(2)}) async-start(), calls=%async_computation.26 | async-start | bytes 3686400 | tf_op jit(solution)/shard_map/reduce_scatter | solution.py:305
  771.7 392.7 %reduce-scatter.35.cloned.1.call-start = ((), (), s32[]{:S(2)}) async-start(), calls=%async_computation.24 | async-start | bytes 3686400 | tf_op jit(solution)/shard_map/reduce_scatter | solution.py:302
  777.0 430.0 %reduce-scatter.31.cloned.1.call-start = ((), (), s32[]{:S(2)}) async-start(), calls=%async_computation.22 | async-start | bytes 3686400 | tf_op jit(solution)/shard_map/reduce_scatter | solution.py:299
  782.1 497.1 %all-reduce.24.cloned.1.call-start = ((), (), s32[]{:S(2)}) async-start(), calls=%async_computation.39 | async-start | bytes 4915200 | tf_op jit(solution)/shard_map/psum | solution.py:322
  952.0 360.4 %reduce-scatter.45.cloned.1.call-start = ((), (), s32[]{:S(2)}) async-start(), calls=%async_computation.37 | async-start | bytes 368640
  953.0 391.0 %reduce-scatter.43.cloned.1.call-start = ((), (), s32[]{:S(2)}) async-start(), calls=%async_computation.36 | async-start | bytes 368640
  962.4 460.4 %all-reduce.22.cloned.1.call-start = ((), (), s32[]{:S(2)}) async-start(), calls=%async_computation.38 | async-start | bytes 4915200 | tf_op jit(solution)/shard_map/psum | solution.py:325
  1207.0 289.0 %all-reduce.26.cloned.1.call-start = ((), (), s32[]{:S(2)}) async-start(), calls=%async_computation.40 | async-start | bytes 4915200 | tf_op jit(solution)/shard_map/psum | solution.py:322
  (67 other events, 725.2 us)
Sparse Core Ops, SparseCore 0:
  10.6 97.2 all-gather.30
  117.8 37.5 all-gather.26
  157.6 40.0 all-gather.32
  199.8 39.3 all-gather.34
  240.6 38.2 all-gather.36
  280.4 92.8 all-gather.38
  383.1 37.4 all-gather.28
  422.2 39.3 all-gather.40
  463.3 38.2 all-gather.42
  503.0 38.2 all-gather.44
  598.5 37.5 reduce-scatter.18
  665.1 37.5 reduce-scatter.24
  705.0 37.5 reduce-scatter.22
  744.8 103.2 reduce-scatter.28
  850.3 101.5 reduce-scatter.26
  954.1 39.6 reduce-scatter.36
  996.7 40.1 reduce-scatter.32
  1039.2 40.1 reduce-scatter.40
  1081.6 40.1 reduce-scatter.38
  1124.2 40.1 reduce-scatter.34
  1166.8 40.1 reduce-scatter.30
  1209.4 69.7 all-reduce.23
  1347.7 75.0 all-reduce.21
  1425.0 70.9 all-reduce.25
  (3 shorter events, 95.4 us)
